TPU v7x, 32 devices: a whole 2x2x4 slice. The times are simulated.
32 devices in a mesh: grp: 2 (over x), tile: 8 (over z, y), wave: 2 (over core).
Axes of the slice: x: 2, y: 2, z: 4, core: 2. Of those that a mesh axis runs over, the one named last changes fastest.
Arguments:
- residual: float32 [16, 8, 2, 8, 128], P(('grp', 'tile'), 'wave'), parts along dimension 0, may hold values from -210 to 210
- kernel: bfloat16 [16, 8, 9, 2, 128, 128], P(('grp', 'tile'), 'wave'), parts along dimension 0, may hold values from -0.125 to 0.125
- offsets: float32 [16, 8, 2, 128], P(('grp', 'tile'), 'wave'), parts along dimension 0, may hold values from 0 to 1
- neighbor: int32 [16, 8, 9], P(('grp', 'tile'), 'wave'), parts along dimension 0, may hold values from 0 to 8, each once within a row
- frequency: int32 [16], P('grp'), parts along dimension 0, may hold values from 0 to 7, each once
- lattice_x: int32 [128], replicated, may hold values from 0 to 127, each once
- lattice_y: int32 [128], replicated, may hold values from 0 to 127, each once
- spectral_weight: float32 [8, 128, 128], replicated, may hold values from 0.1 to 3
Outputs:
- image_two: float32 [16, 8, 2, 8, 128], P(('grp', 'tile'), 'wave'), parts along dimension 0
- arnoldi: float32 [8, 8], P('grp'), parts along dimension 0
There are 2 independent parts, one for each index of `grp`. A program takes and returns all parts, laid end to end along the dimension named above; an argument that names none is the same for every part. Nothing has to cross between parts.
Inputs may be any that keep to these rules, and one draw needn't show every extreme that they name: `neighbor`: each row names each of the nine neighbour slots once. `frequency`: each index appears once. `lattice_x`: each index appears once. `lattice_y`: each index appears once.
All inputs are finite; a program needn't handle non-finite values.
Results may differ from a plain program's by a relative error of at most 0.013.
Values may be sent and summed in bfloat16 or wider, within the bound.
A program may use at most 64 MiB of HBM per device.

v0:
```python
import math
import jax
import jax.numpy as jnp
from jax import lax
from jax.sharding import PartitionSpec as P

two_pi = 2.0 * math.pi
eps_norm = 1e-06


def padded_2(array, sides, width):
    for axis, dim in sides:
        size, length = (lax.axis_size(axis), array.shape[dim])
        up = [(i, (i + 1) % size) for i in range(size)]
        down = [(j, i) for i, j in up]
        last = lax.slice_in_dim(array, length - width, length, axis=dim)
        initial = lax.slice_in_dim(array, 0, width, axis=dim)
        before = lax.ppermute(last, axis, up)
        after = lax.ppermute(initial, axis, down)
        array = jnp.concatenate([before, array, after], axis=dim)
    return array


def phase_table(position, harmonic):
    phase_angle = two_pi * (position[:, None] * harmonic[None, :])
    return (jnp.cos(phase_angle).astype(jnp.bfloat16), jnp.sin(phase_angle).astype(jnp.bfloat16))


def project_rows(cosine_cols, sine_cols, twisted):
    row_count = cosine_cols.shape[1]
    stacked = jnp.concatenate([cosine_cols, sine_cols], 1)
    gram_matrix = lax.dot_general(
        stacked, twisted, (((0,), (0,)), ((), ())), preferred_element_type=jnp.float32
    )
    gram_matrix = gram_matrix.reshape(2, row_count, 2, -1)
    coef_real = gram_matrix[0, :, 0] + gram_matrix[1, :, 1]
    coef_imag = gram_matrix[0, :, 1] - gram_matrix[1, :, 0]
    return jnp.stack([coef_real, coef_imag], 1)


def expand_rows(cosine_cols, sine_cols, scaled):
    row_count = scaled.shape[0]
    upper_rows = scaled.reshape(row_count, -1)
    lower_rows = jnp.stack([-scaled[:, 1], scaled[:, 0]], 1).reshape(row_count, -1)
    matrix = jnp.concatenate([upper_rows, lower_rows], 0)
    stacked = jnp.concatenate([cosine_cols, sine_cols], 1)
    return jnp.dot(stacked, matrix, preferred_element_type=jnp.float32)


def twist_density(panel_density, cosine_y, sine_y):
    density_real = panel_density[:, 0, :, None].astype(jnp.float32)
    density_imag = panel_density[:, 1, :, None].astype(jnp.float32)
    wave_cos = cosine_y.astype(jnp.float32)[:, None, :]
    wave_sin = sine_y.astype(jnp.float32)[:, None, :]
    part_real = wave_cos * density_real + wave_sin * density_imag
    part_imag = wave_cos * density_imag - wave_sin * density_real
    return (
        jnp.stack([part_real, part_imag], 1)
        .reshape(panel_density.shape[0], -1)
        .astype(jnp.bfloat16)
    )


def finish(summed, cosine_y, sine_y, vectors):
    shaped = summed.reshape(summed.shape[0], 2, vectors, -1)
    wave_cos = cosine_y.astype(jnp.float32)[:, None, :]
    wave_sin = sine_y.astype(jnp.float32)[:, None, :]
    far_real = jnp.sum(shaped[:, 0] * wave_cos - shaped[:, 1] * wave_sin, -1)
    far_imag = jnp.sum(shaped[:, 0] * wave_sin + shaped[:, 1] * wave_cos, -1)
    return jnp.stack([far_real, far_imag], 1)


def combine_near(product, vectors):
    first_half = product[:, 0]
    second = product[:, 1]
    near_real = first_half[:, :vectors] - second[:, vectors:]
    near_imag = second[:, :vectors] + first_half[:, vectors:]
    return jnp.stack([near_real, near_imag], 1)


def panel_sum(values):
    return jnp.sum(values, axis=(0, 1, 3))


def per_device(
    residual, kernel, offsets, neighbor, frequency, lattice_x, lattice_y, spectral_weight
):
    strips = residual.shape[0]
    tiles_y = residual.shape[1]
    vectors = residual.shape[3]
    panels_t = residual.shape[4]
    modes_x = spectral_weight.shape[1]
    modes_y = spectral_weight.shape[2]
    count_x = lax.axis_size("tile") * strips
    count_y = lax.axis_size("wave") * tiles_y
    devices = lax.axis_size("tile") * lax.axis_size("wave")
    panels = count_x * count_y * panels_t
    local_rows = strips * tiles_y * panels_t
    column = (lax.axis_index("tile") * strips + jnp.arange(strips)).astype(jnp.float32)
    row_index = (lax.axis_index("wave") * tiles_y + jnp.arange(tiles_y)).astype(jnp.float32)
    position_x = ((column[:, None, None] + offsets[:, :, 0, :]) / count_x).reshape(-1)
    position_y = ((row_index[None, :, None] + offsets[:, :, 1, :]) / count_y).reshape(-1)
    harmonic_x = (lattice_x - modes_x // 2).astype(jnp.float32)
    harmonic_y = (lattice_y - modes_y // 2).astype(jnp.float32)
    cosine_x, sine_x = phase_table(position_x, harmonic_x)
    cosine_y, sine_y = phase_table(position_y, harmonic_y)
    weight_rows = jnp.take(spectral_weight, frequency, axis=0)
    factor = weight_rows * (1.0 / math.sqrt(modes_x * modes_y * panels))
    factor_wide = jnp.transpose(factor, (1, 0, 2)).reshape(modes_x, vectors * modes_y)[:, None, :]

    def near_field(density):
        padded = padded_2(density, (("tile", 0), ("wave", 1)), 1)
        candidates = []
        for slot_index in range(9):
            shift_x = slot_index // 3 - 1
            shift_y = slot_index % 3 - 1
            candidates.append(
                padded[1 + shift_x : 1 + shift_x + strips, 1 + shift_y : 1 + shift_y + tiles_y]
            )
        stacked = jnp.stack(candidates, 2).reshape(strips * tiles_y, 9, -1)
        picked = jnp.take_along_axis(stacked, neighbor.reshape(strips * tiles_y, 9, 1), axis=1)
        picked = picked.reshape(strips * tiles_y, 9, 2 * vectors, panels_t)
        blocks = kernel.reshape(strips * tiles_y, 9, 2, panels_t, panels_t)
        product = jnp.einsum("tjmp,tjcpq->tcmq", picked, blocks, preferred_element_type=jnp.float32)
        return combine_near(product, vectors).reshape(strips, tiles_y, 2, vectors, panels_t)

    def far_field(density):
        panel_density = jnp.transpose(density, (0, 1, 4, 2, 3)).reshape(local_rows, 2, vectors)
        twisted = twist_density(panel_density, cosine_y, sine_y)
        partial_coeffs = project_rows(cosine_x, sine_x, twisted)
        share_rows = modes_x // devices
        shares = lax.psum_scatter(partial_coeffs, ("tile", "wave"), scatter_dimension=0, tiled=True)
        owner_index = lax.axis_index("tile") * lax.axis_size("wave") + lax.axis_index("wave")
        owner_factor = lax.dynamic_slice_in_dim(
            factor_wide, owner_index * share_rows, share_rows, 0
        )
        owner_scaled = (shares * owner_factor).astype(jnp.bfloat16)
        scaled = lax.all_gather(owner_scaled, ("tile", "wave"), axis=0, tiled=True)
        summed = expand_rows(cosine_x, sine_x, scaled)
        far_panel = finish(summed, cosine_y, sine_y, vectors)
        return far_panel.reshape(strips, tiles_y, panels_t, 2, vectors).transpose(0, 1, 3, 4, 2)

    def apply_operator(density):
        return 0.5 * density.astype(jnp.float32) + near_field(density) + far_field(density)

    local_sq = panel_sum(
        residual[:, :, 0] * residual[:, :, 0] + residual[:, :, 1] * residual[:, :, 1]
    )
    squares = lax.psum(local_sq, ("tile", "wave"))
    basis_scale = jnp.sqrt(squares / panels + eps_norm)
    basis_one = (residual / basis_scale[None, None, None, :, None]).astype(jnp.bfloat16)
    image_one = apply_operator(basis_one)
    basis_real = basis_one[:, :, 0].astype(jnp.float32)
    basis_imag = basis_one[:, :, 1].astype(jnp.float32)
    image_real = image_one[:, :, 0]
    image_imag = image_one[:, :, 1]
    inner_real, inner_imag = lax.psum(
        (
            panel_sum(basis_real * image_real + basis_imag * image_imag),
            panel_sum(basis_real * image_imag - basis_imag * image_real),
        ),
        ("tile", "wave"),
    )
    coef_real = inner_real / panels
    coef_imag = inner_imag / panels
    wide_real = coef_real[None, None, :, None]
    wide_imag = coef_imag[None, None, :, None]
    update_real = image_real - (wide_real * basis_real - wide_imag * basis_imag)
    update_imag = image_imag - (wide_real * basis_imag + wide_imag * basis_real)
    update_sq = lax.psum(
        panel_sum(update_real * update_real + update_imag * update_imag), ("tile", "wave")
    )
    update_scale = jnp.sqrt(update_sq / panels + eps_norm)
    next_basis = (
        jnp.stack([update_real, update_imag], 2) / update_scale[None, None, None, :, None]
    ).astype(jnp.bfloat16)
    image_two = apply_operator(next_basis)
    arnoldi = jnp.stack([basis_scale, coef_real, coef_imag, update_scale])
    return (image_two, arnoldi)


def solution(mesh):
    return jax.shard_map(
        per_device,
        mesh=mesh,
        in_specs=(
            P(("grp", "tile"), "wave", None, None, None),
            P(("grp", "tile"), "wave", None, None, None, None),
            P(("grp", "tile"), "wave", None, None),
            P(("grp", "tile"), "wave", None),
            P("grp"),
            P(),
            P(),
            P(),
        ),
        out_specs=(P(("grp", "tile"), "wave", None, None, None), P("grp", None)),
        check_vma=False,
    )
```

profile of v0, /device:TPU:0, one launch (start us, length us, event | category | flops | bytes accessed | tf_op | source)
XLA Modules:
  0.0 307.0 jit_solution(9363511399105179548)
XLA Ops:
  8.2 34.9 %psum.28 = f32[8]{0:T(128)S(1)} all-reduce(f32[8]{0:T(128)S(1)} %add_reduce_fusion.2), channel_id=1, replica_groups=mesh['grp'=2,'tile'=8,'wave'=2] {'tile','wave'}, use_global_device_ids=true, to_apply=%region_1.2 | all-reduce | flops 8 | bytes 64 | tf_op jit(solution)/shard_map/psum | solution.py:149
  43.7 1.4 fusion.22
  45.2 4.7 %collective-permute-start.1 = (bf16[1,4,2,8,128]{4,3,1,2,0:T(8,128)(2,1)}, bf16[1,4,2,8,128]{4,3,1,2,0:T(8,128)(2,1)}, u32[]{:S(2)}, u32[]{:S(2)}) collective-permute-start(bf16[1,4,2,8,128]{4,3,1,2,0:T(8,128)(2,1)} %fusion.22), channel_id=1, source_target_pairs={{2,0},{4,2},{6,4},{8,6},{10,8},{12,10},{14,12},{0,14},{3,1},{5,3},... | collective-permute-start | bytes 49160 | tf_op jit(solution)/shard_map/ppermute | solution.py:19
  54.7 1.1 cosine_convert_fusion.1
  56.9 1.1 pad_maximum_fusion.2
  58.7 1.6 gather_fusion
  61.7 1.2 copy.121
  63.0 1.3 pad_maximum_fusion.31
  67.8 1.2 copy.122
  73.7 1.5 gather_fusion.1
  76.5 36.3 %reduce-scatter.3.cloned.1.call-done = f32[8,2,1024]{2,0,1:T(8,128)} async-done(((f32[128,2,1024]{2,0,1:T(8,128)}), f32[8,2,1024]{2,0,1:T(8,128)}) %reduce-scatter.3.cloned.1.call-update) | async-done | bytes 65552 | tf_op jit(solution)/shard_map/reduce_scatter | solution.py:132
  113.7 20.8 %all_gather.6 = bf16[128,2,1024]{2,0,1:T(8,128)(2,1)S(1)} all-gather(bf16[8,2,1024]{2,0,1:T(8,128)(2,1)S(1)} %multiply_convert_fusion.1), channel_id=1, replica_groups=mesh['grp'=2,'tile'=8,'wave'=2] {'tile','wave'}, dimensions={0}, use_global_device_ids=true | all-gather | bytes 557056 | tf_op jit(solution)/shard_map/all_gather | solution.py:138
  136.3 1.1 pad_maximum_fusion.4
  138.4 2.0 convolution_bitcast_fusion.1
  141.4 1.2 subtract_reduce_fusion.1
  145.2 29.8 %all-reduce = (f32[8]{0:T(128)S(1)}, f32[8]{0:T(128)S(1)}) all-reduce(f32[8]{0:T(128)S(1)} %get-tuple-element.16, f32[8]{0:T(128)S(1)} %get-tuple-element.15), channel_id=1, replica_groups=mesh['grp'=2,'tile'=8,'wave'=2] {'tile','wave'}, use_global_device_ids=true, to_apply=%region_8.10 | all-reduce | flops 16 | bytes 128 | tf_op jit(solution)/shard_map/psum | solution.py:157
  176.7 29.5 %psum.31 = f32[8]{0:T(128)S(1)} all-reduce(f32[8]{0:T(128)S(1)} %fusion.40), channel_id=1, replica_groups=mesh['grp'=2,'tile'=8,'wave'=2] {'tile','wave'}, use_global_device_ids=true, to_apply=%region_10.12 | all-reduce | flops 8 | bytes 64 | tf_op jit(solution)/shard_map/psum | solution.py:170
  206.4 4.7 %collective-permute-start.5 = (bf16[1,4,2,8,128]{4,3,1,2,0:T(8,128)(2,1)S(1)}, bf16[1,4,2,8,128]{4,3,1,2,0:T(8,128)(2,1)S(1)}, u32[]{:S(2)}, u32[]{:S(2)}) collective-permute-start(bf16[1,4,2,8,128]{4,3,1,2,0:T(8,128)(2,1)S(1)} %fusion.20), channel_id=1, source_target_pairs={{2,0},{4,2},{6,4},{8,6},{10,8},{12,10},{14,12},{0,14},{3,1},{5,3},... | collective-permute-start | bytes 49160 | tf_op jit(solution)/shard_map/ppermute | solution.py:19
  213.7 1.1 pad_maximum_fusion.3
  217.2 1.5 gather_fusion.2
  219.4 50.2 %reduce-scatter.5.cloned.1.call-done = f32[8,2,1024]{2,0,1:T(8,128)} async-done(((f32[128,2,1024]{2,0,1:T(8,128)}), f32[8,2,1024]{2,0,1:T(8,128)}) %reduce-scatter.5.cloned.1.call-update) | async-done | bytes 65552 | tf_op jit(solution)/shard_map/reduce_scatter | solution.py:132
  270.5 20.8 %all_gather.7 = bf16[128,2,1024]{2,0,1:T(8,128)(2,1)S(1)} all-gather(bf16[8,2,1024]{2,0,1:T(8,128)(2,1)S(1)} %multiply_convert_fusion), channel_id=1, replica_groups=mesh['grp'=2,'tile'=8,'wave'=2] {'tile','wave'}, dimensions={0}, use_global_device_ids=true | all-gather | bytes 557056 | tf_op jit(solution)/shard_map/all_gather | solution.py:138
  295.1 2.0 convolution_bitcast_fusion
  298.1 1.2 subtract_reduce_fusion
  (197 shorter events, 39.9 us)
Async XLA Ops:
  7.2 68.3 %copy-start = (bf16[1,4,9,2,128,128]{5,4,3,2,1,0:T(8,128)(2,1)S(1)}, bf16[1,4,9,2,128,128]{5,4,3,2,1,0:T(8,128)(2,1)}, u32[]{:S(2)}) copy-start(bf16[1,4,9,2,128,128]{5,4,3,2,1,0:T(8,128)(2,1)} %param.11) | copy-start | bytes 7077892
  7.2 105.6 %reduce-scatter.3.cloned.1.call-start = ((), (), s32[]{:S(2)}) async-start(), calls=%async_computation.2 | async-start | bytes 1114112 | tf_op jit(solution)/shard_map/reduce_scatter | solution.py:132
  43.7 7.0 %copy-start.19 = (f32[8]{0:T(128)}, f32[8]{0:T(128)S(1)}, u32[]{:S(2)}) copy-start(f32[8]{0:T(128)S(1)} %get-tuple-element.68) | copy-start | bytes 100
  45.2 17.8 %collective-permute-start = (bf16[1,4,2,8,128]{4,3,1,2,0:T(8,128)(2,1)}, bf16[1,4,2,8,128]{4,3,1,2,0:T(8,128)(2,1)}, u32[]{:S(2)}, u32[]{:S(2)}) collective-permute-start(bf16[1,4,2,8,128]{4,3,1,2,0:T(8,128)(2,1)} %fusion.22), channel_id=1, source_target_pairs={{0,2},{2,4},{4,6},{6,8},{8,10},{10,12},{12,14},{14,0},{1,3},{3,5},... | collective-permute-start | bytes 49160 | tf_op jit(solution)/shard_map/ppermute | solution.py:18
  45.2 17.8 %collective-permute-start.1 = (bf16[1,4,2,8,128]{4,3,1,2,0:T(8,128)(2,1)}, bf16[1,4,2,8,128]{4,3,1,2,0:T(8,128)(2,1)}, u32[]{:S(2)}, u32[]{:S(2)}) collective-permute-start(bf16[1,4,2,8,128]{4,3,1,2,0:T(8,128)(2,1)} %fusion.22), channel_id=1, source_target_pairs={{2,0},{4,2},{6,4},{8,6},{10,8},{12,10},{14,12},{0,14},{3,1},{5,3},... | collective-permute-start | bytes 49160 | tf_op jit(solution)/shard_map/ppermute | solution.py:19
  53.9 12.3 %copy-start.1 = (f32[512,128]{0,1:T(8,128)}, f32[512,128]{0,1:T(8,128)S(1)}, u32[]{:S(2)}) copy-start(f32[512,128]{0,1:T(8,128)S(1)} %get-tuple-element.64) | copy-start | bytes 786436
  58.0 211.7 %reduce-scatter.5.cloned.1.call-start = ((), (), s32[]{:S(2)}) async-start(), calls=%async_computation.3 | async-start | bytes 1114112 | tf_op jit(solution)/shard_map/reduce_scatter | solution.py:132
  64.3 7.5 %collective-permute-start.2 = (bf16[3,1,2,8,128]{4,3,1,2,0:T(8,128)(2,1)}, bf16[3,1,2,8,128]{4,3,1,2,0:T(8,128)(2,1)}, u32[]{:S(2)}, u32[]{:S(2)}) collective-permute-start(bf16[3,1,2,8,128]{4,3,1,2,0:T(8,128)(2,1)} %get-tuple-element.56), channel_id=1, source_target_pairs={{0,1},{1,0},{2,3},{3,2},{4,5},{5,4},{6,7},{7,6},{8,9},{9,8},{10,11... | collective-permute-start | bytes 36872 | tf_op jit(solution)/shard_map/ppermute | solution.py:18
  67.7 7.5 %copy-start.21 = (pred[4,9]{1,0:T(4,128)(4,1)S(1)}, pred[4,9]{1,0:T(4,128)(4,1)}, u32[]{:S(2)}) copy-start(pred[4,9]{1,0:T(4,128)(4,1)} %and_bitcast_fusion) | copy-start | bytes 112
  69.0 43.9 %copy-start.16 = (f32[8,1,1024]{2,0,1:T(8,128)}, f32[8,1,1024]{2,0,1:T(8,128)S(1)}, u32[]{:S(2)}) copy-start(f32[8,1,1024]{2,0,1:T(8,128)S(1)} %copy.122) | copy-start | bytes 98308
  70.5 2.1 collective-permute-start.3
  134.4 4.0 %copy-start.10 = (bf16[512,128]{0,1:T(8,128)(2,1)S(1)}, bf16[512,128]{0,1:T(8,128)(2,1)}, u32[]{:S(2)}) copy-start(bf16[512,128]{0,1:T(8,128)(2,1)} %copy-done.9) | copy-start | bytes 393220
  141.4 2.0 copy-start.20
  141.4 69.8 %copy-start.2 = (f32[512,128]{0,1:T(8,128)S(1)}, f32[512,128]{0,1:T(8,128)}, u32[]{:S(2)}) copy-start(f32[512,128]{0,1:T(8,128)} %copy-done.1) | copy-start | bytes 786436
  176.7 38.0 %copy-start.12 = (f32[1,4,1,8,128]{4,3,1,2,0:T(8,128)}, f32[1,4,1,8,128]{4,3,1,2,0:T(8,128)S(1)}, u32[]{:S(2)}) copy-start(f32[1,4,1,8,128]{4,3,1,2,0:T(8,128)S(1)} %get-tuple-element.51) | copy-start | bytes 49156
  176.7 38.0 %copy-start.14 = (f32[1,4,1,8,128]{4,3,1,2,0:T(8,128)}, f32[1,4,1,8,128]{4,3,1,2,0:T(8,128)S(1)}, u32[]{:S(2)}) copy-start(f32[1,4,1,8,128]{4,3,1,2,0:T(8,128)S(1)} %get-tuple-element.52) | copy-start | bytes 49156
  206.4 8.4 %collective-permute-start.4 = (bf16[1,4,2,8,128]{4,3,1,2,0:T(8,128)(2,1)S(1)}, bf16[1,4,2,8,128]{4,3,1,2,0:T(8,128)(2,1)S(1)}, u32[]{:S(2)}, u32[]{:S(2)}) collective-permute-start(bf16[1,4,2,8,128]{4,3,1,2,0:T(8,128)(2,1)S(1)} %fusion.20), channel_id=1, source_target_pairs={{0,2},{2,4},{4,6},{6,8},{8,10},{10,12},{12,14},{14,0},{1,3},{3,5},... | collective-permute-start | bytes 49160 | tf_op jit(solution)/shard_map/ppermute | solution.py:18
  206.4 8.4 %collective-permute-start.5 = (bf16[1,4,2,8,128]{4,3,1,2,0:T(8,128)(2,1)S(1)}, bf16[1,4,2,8,128]{4,3,1,2,0:T(8,128)(2,1)S(1)}, u32[]{:S(2)}, u32[]{:S(2)}) collective-permute-start(bf16[1,4,2,8,128]{4,3,1,2,0:T(8,128)(2,1)S(1)} %fusion.20), channel_id=1, source_target_pairs={{2,0},{4,2},{6,4},{8,6},{10,8},{12,10},{14,12},{0,14},{3,1},{5,3},... | collective-permute-start | bytes 49160 | tf_op jit(solution)/shard_map/ppermute | solution.py:19
  214.8 4.0 %copy-start.22 = (pred[4,9]{1,0:T(4,128)(4,1)S(1)}, pred[4,9]{1,0:T(4,128)(4,1)}, u32[]{:S(2)}) copy-start(pred[4,9]{1,0:T(4,128)(4,1)} %and_bitcast_fusion) | copy-start | bytes 112
  214.8 1.2 collective-permute-start.7
  215.5 1.3 collective-permute-start.6
  218.7 51.0 %copy-start.17 = (f32[8,1,1024]{2,0,1:T(8,128)S(1)}, f32[8,1,1024]{2,0,1:T(8,128)}, u32[]{:S(2)}) copy-start(f32[8,1,1024]{2,0,1:T(8,128)} %copy-done.16) | copy-start | bytes 98308
  291.3 3.8 %copy-start.11 = (bf16[512,128]{0,1:T(8,128)(2,1)S(1)}, bf16[512,128]{0,1:T(8,128)(2,1)}, u32[]{:S(2)}) copy-start(bf16[512,128]{0,1:T(8,128)(2,1)} %copy-done.9) | copy-start | bytes 393220
  298.0 1.4 copy-start.15
  (11 other events, 11.5 us)
Sparse Core Ops, SparseCore 0:
  58.1 54.6 reduce-scatter.2
  214.9 54.7 reduce-scatter.4
where the time goes:
time: 308 us; the launch traced here: 307 us
  blocking collectives  136 us (44%)
  waiting for transfers between devices  87.3 us (28%)
  other arithmetic  30 us (10%)
  local copies, waits for them, and re-layouts  22.2 us (7%)
  between operations  14.9 us (5%)
  starting transfers between devices  10.7 us (3%)
  matrix products  6.26 us (2%)
    reduce_scatter x2, waiting for transfers between devices, far_field(): lax.psum_scatter(partial_coeffs, ('tile', 'wave'), scatter_dimension=0, t...  86.5 us
    all_gather x2, blocking collectives, far_field(): scaled = lax.all_gather(owner_scaled, ('tile', 'wave'), axis=0, tiled=True)  41.5 us
    psum x1, blocking collectives, per_device(): squares = lax.psum(local_sq, ('tile', 'wave'))  34.9 us
    psum x1, blocking collectives, per_device(): lax.psum((panel_sum(basis_real * image_real + basis_imag * image_imag), p...  29.8 us
    psum x1, blocking collectives, per_device(): lax.psum(panel_sum(update_real * update_real + update_imag * update_imag)...  29.5 us
    ppermute x4, starting transfers between devices, padded_2(): after = lax.ppermute(initial, axis, down)  10.1 us
  transfers between devices with their start and end apart: 10, of which 3 were waited for; matrix products, arithmetic and copies ran while one was open for 10% of the time, Pallas kernels for 0%

commit v1 on v0

--- a/solution.py
+++ b/solution.py
@@ -167,9 +167,9 @@
     wide_imag = coef_imag[None, None, :, None]
     update_real = image_real - (wide_real * basis_real - wide_imag * basis_imag)
     update_imag = image_imag - (wide_real * basis_imag + wide_imag * basis_real)
-    update_sq = lax.psum(
-        panel_sum(update_real * update_real + update_imag * update_imag), ("tile", "wave")
-    )
+    block = panel_sum(update_real * update_real + update_imag * update_imag)
+    shards = lax.all_gather(block, ("tile", "wave"), axis=0, tiled=False)
+    update_sq = shards.sum(axis=0)
     update_scale = jnp.sqrt(update_sq / panels + eps_norm)
     next_basis = (
         jnp.stack([update_real, update_imag], 2) / update_scale[None, None, None, :, None]

time: 308 us -> 309 us (level)
    psum x1 -> x0, blocking collectives: 29.5 us -> none  [per_device(): lax.psum(panel_sum(update_real * update_real + update_imag * update_imag)...]
    unnamed x0 -> x1, blocking collectives: none -> 29.5 us
  transfers between devices with their start and end apart: 10 -> 10, of which waited for: 3 -> 3; matrix products, arithmetic and copies ran while one was open for 10% -> 11% of each run, Pallas kernels for 0% -> 0%
where the time goes in v1:
time: 309 us; the launch traced here: 307 us
  blocking collectives  136 us (44%)
  waiting for transfers between devices  85.4 us (28%)
  other arithmetic  30.1 us (10%)
  local copies, waits for them, and re-layouts  23.7 us (8%)
  between operations  15.5 us (5%)
  starting transfers between devices  10.7 us (3%)
  matrix products  6.25 us (2%)
    reduce_scatter x2, waiting for transfers between devices, far_field(): lax.psum_scatter(partial_coeffs, ('tile', 'wave'), scatter_dimension=0, t...  84.6 us
    all_gather x2, blocking collectives, far_field(): scaled = lax.all_gather(owner_scaled, ('tile', 'wave'), axis=0, tiled=True)  41.5 us
    psum x1, blocking collectives, per_device(): squares = lax.psum(local_sq, ('tile', 'wave'))  34.9 us
    psum x1, blocking collectives, per_device(): lax.psum((panel_sum(basis_real * image_real + basis_imag * image_imag), p...  29.8 us
    unnamed x1, blocking collectives  29.5 us
    ppermute x4, starting transfers between devices, padded_2(): after = lax.ppermute(initial, axis, down)  10.1 us
  transfers between devices with their start and end apart: 10, of which 3 were waited for; matrix products, arithmetic and copies ran while one was open for 11% of the time, Pallas kernels for 0%

profile of v1, /device:TPU:0, one launch (start us, length us, event | category | flops | bytes accessed | tf_op | source)
XLA Modules:
  0.0 307.4 jit_solution(2859932578354448934)
XLA Ops:
  8.2 34.9 %psum.21 = f32[8]{0:T(128)S(1)} all-reduce(f32[8]{0:T(128)S(1)} %add_reduce_fusion.2), channel_id=1, replica_groups=mesh['grp'=2,'tile'=8,'wave'=2] {'tile','wave'}, use_global_device_ids=true, to_apply=%region_1.2 | all-reduce | flops 8 | bytes 64 | tf_op jit(solution)/shard_map/psum | solution.py:149
  43.7 1.4 fusion.22
  45.2 4.7 %collective-permute-start.1 = (bf16[1,4,2,8,128]{4,3,1,2,0:T(8,128)(2,1)}, bf16[1,4,2,8,128]{4,3,1,2,0:T(8,128)(2,1)}, u32[]{:S(2)}, u32[]{:S(2)}) collective-permute-start(bf16[1,4,2,8,128]{4,3,1,2,0:T(8,128)(2,1)} %fusion.22), channel_id=1, source_target_pairs={{2,0},{4,2},{6,4},{8,6},{10,8},{12,10},{14,12},{0,14},{3,1},{5,3},... | collective-permute-start | bytes 49160 | tf_op jit(solution)/shard_map/ppermute | solution.py:19
  54.7 1.1 cosine_convert_fusion.1
  56.9 1.1 pad_maximum_fusion.2
  58.7 1.6 gather_fusion
  61.8 1.2 copy.121
  63.1 1.3 pad_maximum_fusion.31
  67.8 1.2 copy.122
  69.9 1.2 dynamic-slice
  75.7 1.5 gather_fusion.1
  78.5 34.4 %reduce-scatter.3.cloned.1.call-done = f32[8,2,1024]{2,0,1:T(8,128)} async-done(((f32[128,2,1024]{2,0,1:T(8,128)}), f32[8,2,1024]{2,0,1:T(8,128)}) %reduce-scatter.3.cloned.1.call-update) | async-done | bytes 65552 | tf_op jit(solution)/shard_map/reduce_scatter | solution.py:132
  113.8 20.7 %all_gather.12 = bf16[128,2,1024]{2,0,1:T(8,128)(2,1)S(1)} all-gather(bf16[8,2,1024]{2,0,1:T(8,128)(2,1)S(1)} %multiply_convert_fusion.1), channel_id=1, replica_groups=mesh['grp'=2,'tile'=8,'wave'=2] {'tile','wave'}, dimensions={0}, use_global_device_ids=true | all-gather | bytes 557056 | tf_op jit(solution)/shard_map/all_gather | solution.py:138
  138.5 2.0 convolution_bitcast_fusion.1
  141.5 1.2 subtract_reduce_fusion.1
  145.3 29.8 %all-reduce.1 = (f32[8]{0:T(128)S(1)}, f32[8]{0:T(128)S(1)}) all-reduce(f32[8]{0:T(128)S(1)} %get-tuple-element.16, f32[8]{0:T(128)S(1)} %get-tuple-element.15), channel_id=1, replica_groups=mesh['grp'=2,'tile'=8,'wave'=2] {'tile','wave'}, use_global_device_ids=true, to_apply=%region_8.10 | all-reduce | flops 16 | bytes 128 | tf_op jit(solution)/shard_map/psum | solution.py:157
  177.0 29.5 %all-reduce = f32[128]{0:T(128)S(1)} all-reduce(f32[128]{0:T(128)S(1)} %dynamic-update-slice), channel_id=2, replica_groups=mesh['grp'=2,'tile'=8,'wave'=2] {'tile','wave'}, use_global_device_ids=true, to_apply=%add | all-reduce | flops 128 | bytes 1024
  206.8 4.7 %collective-permute-start.5 = (bf16[1,4,2,8,128]{4,3,1,2,0:T(8,128)(2,1)S(1)}, bf16[1,4,2,8,128]{4,3,1,2,0:T(8,128)(2,1)S(1)}, u32[]{:S(2)}, u32[]{:S(2)}) collective-permute-start(bf16[1,4,2,8,128]{4,3,1,2,0:T(8,128)(2,1)S(1)} %fusion.20), channel_id=1, source_target_pairs={{2,0},{4,2},{6,4},{8,6},{10,8},{12,10},{14,12},{0,14},{3,1},{5,3},... | collective-permute-start | bytes 49160 | tf_op jit(solution)/shard_map/ppermute | solution.py:19
  214.1 1.1 pad_maximum_fusion.3
  217.6 1.5 gather_fusion.2
  219.8 50.2 %reduce-scatter.5.cloned.1.call-done = f32[8,2,1024]{2,0,1:T(8,128)} async-done(((f32[128,2,1024]{2,0,1:T(8,128)}), f32[8,2,1024]{2,0,1:T(8,128)}) %reduce-scatter.5.cloned.1.call-update) | async-done | bytes 65552 | tf_op jit(solution)/shard_map/reduce_scatter | solution.py:132
  270.9 20.8 %all_gather.15 = bf16[128,2,1024]{2,0,1:T(8,128)(2,1)S(1)} all-gather(bf16[8,2,1024]{2,0,1:T(8,128)(2,1)S(1)} %multiply_convert_fusion), channel_id=1, replica_groups=mesh['grp'=2,'tile'=8,'wave'=2] {'tile','wave'}, dimensions={0}, use_global_device_ids=true | all-gather | bytes 557056 | tf_op jit(solution)/shard_map/all_gather | solution.py:138
  295.4 2.0 convolution_bitcast_fusion
  298.4 1.2 subtract_reduce_fusion
  (202 shorter events, 41.4 us)
Async XLA Ops:
  7.2 70.3 %copy-start = (bf16[1,4,9,2,128,128]{5,4,3,2,1,0:T(8,128)(2,1)S(1)}, bf16[1,4,9,2,128,128]{5,4,3,2,1,0:T(8,128)(2,1)}, u32[]{:S(2)}) copy-start(bf16[1,4,9,2,128,128]{5,4,3,2,1,0:T(8,128)(2,1)} %param.11) | copy-start | bytes 7077892
  7.2 105.7 %reduce-scatter.3.cloned.1.call-start = ((), (), s32[]{:S(2)}) async-start(), calls=%async_computation.2 | async-start | bytes 1114112 | tf_op jit(solution)/shard_map/reduce_scatter | solution.py:132
  43.7 7.0 %copy-start.19 = (f32[8]{0:T(128)}, f32[8]{0:T(128)S(1)}, u32[]{:S(2)}) copy-start(f32[8]{0:T(128)S(1)} %get-tuple-element.68) | copy-start | bytes 100
  45.2 17.9 %collective-permute-start = (bf16[1,4,2,8,128]{4,3,1,2,0:T(8,128)(2,1)}, bf16[1,4,2,8,128]{4,3,1,2,0:T(8,128)(2,1)}, u32[]{:S(2)}, u32[]{:S(2)}) collective-permute-start(bf16[1,4,2,8,128]{4,3,1,2,0:T(8,128)(2,1)} %fusion.22), channel_id=1, source_target_pairs={{0,2},{2,4},{4,6},{6,8},{8,10},{10,12},{12,14},{14,0},{1,3},{3,5},... | collective-permute-start | bytes 49160 | tf_op jit(solution)/shard_map/ppermute | solution.py:18
  45.2 17.9 %collective-permute-start.1 = (bf16[1,4,2,8,128]{4,3,1,2,0:T(8,128)(2,1)}, bf16[1,4,2,8,128]{4,3,1,2,0:T(8,128)(2,1)}, u32[]{:S(2)}, u32[]{:S(2)}) collective-permute-start(bf16[1,4,2,8,128]{4,3,1,2,0:T(8,128)(2,1)} %fusion.22), channel_id=1, source_target_pairs={{2,0},{4,2},{6,4},{8,6},{10,8},{12,10},{14,12},{0,14},{3,1},{5,3},... | collective-permute-start | bytes 49160 | tf_op jit(solution)/shard_map/ppermute | solution.py:19
  53.9 12.4 %copy-start.1 = (f32[512,128]{0,1:T(8,128)}, f32[512,128]{0,1:T(8,128)S(1)}, u32[]{:S(2)}) copy-start(f32[512,128]{0,1:T(8,128)S(1)} %get-tuple-element.64) | copy-start | bytes 786436
  58.0 212.0 %reduce-scatter.5.cloned.1.call-start = ((), (), s32[]{:S(2)}) async-start(), calls=%async_computation.3 | async-start | bytes 1114112 | tf_op jit(solution)/shard_map/reduce_scatter | solution.py:132
  64.4 9.4 %collective-permute-start.2 = (bf16[3,1,2,8,128]{4,3,1,2,0:T(8,128)(2,1)}, bf16[3,1,2,8,128]{4,3,1,2,0:T(8,128)(2,1)}, u32[]{:S(2)}, u32[]{:S(2)}) collective-permute-start(bf16[3,1,2,8,128]{4,3,1,2,0:T(8,128)(2,1)} %get-tuple-element.56), channel_id=1, source_target_pairs={{0,1},{1,0},{2,3},{3,2},{4,5},{5,4},{6,7},{7,6},{8,9},{9,8},{10,11... | collective-permute-start | bytes 36872 | tf_op jit(solution)/shard_map/ppermute | solution.py:18
  67.8 9.4 %copy-start.21 = (pred[4,9]{1,0:T(4,128)(4,1)S(1)}, pred[4,9]{1,0:T(4,128)(4,1)}, u32[]{:S(2)}) copy-start(pred[4,9]{1,0:T(4,128)(4,1)} %and_bitcast_fusion) | copy-start | bytes 112
  69.1 43.8 %copy-start.16 = (f32[8,1,1024]{2,0,1:T(8,128)}, f32[8,1,1024]{2,0,1:T(8,128)S(1)}, u32[]{:S(2)}) copy-start(f32[8,1,1024]{2,0,1:T(8,128)S(1)} %copy.122) | copy-start | bytes 98308
  72.5 2.1 collective-permute-start.3
  134.5 4.0 %copy-start.10 = (bf16[512,128]{0,1:T(8,128)(2,1)S(1)}, bf16[512,128]{0,1:T(8,128)(2,1)}, u32[]{:S(2)}) copy-start(bf16[512,128]{0,1:T(8,128)(2,1)} %copy-done.9) | copy-start | bytes 393220
  141.5 2.0 copy-start.20
  141.5 70.1 %copy-start.2 = (f32[512,128]{0,1:T(8,128)S(1)}, f32[512,128]{0,1:T(8,128)}, u32[]{:S(2)}) copy-start(f32[512,128]{0,1:T(8,128)} %copy-done.1) | copy-start | bytes 786436
  176.8 38.4 %copy-start.12 = (f32[1,4,1,8,128]{4,3,1,2,0:T(8,128)}, f32[1,4,1,8,128]{4,3,1,2,0:T(8,128)S(1)}, u32[]{:S(2)}) copy-start(f32[1,4,1,8,128]{4,3,1,2,0:T(8,128)S(1)} %get-tuple-element.51) | copy-start | bytes 49156
  176.8 38.4 %copy-start.14 = (f32[1,4,1,8,128]{4,3,1,2,0:T(8,128)}, f32[1,4,1,8,128]{4,3,1,2,0:T(8,128)S(1)}, u32[]{:S(2)}) copy-start(f32[1,4,1,8,128]{4,3,1,2,0:T(8,128)S(1)} %get-tuple-element.52) | copy-start | bytes 49156
  206.8 8.4 %collective-permute-start.4 = (bf16[1,4,2,8,128]{4,3,1,2,0:T(8,128)(2,1)S(1)}, bf16[1,4,2,8,128]{4,3,1,2,0:T(8,128)(2,1)S(1)}, u32[]{:S(2)}, u32[]{:S(2)}) collective-permute-start(bf16[1,4,2,8,128]{4,3,1,2,0:T(8,128)(2,1)S(1)} %fusion.20), channel_id=1, source_target_pairs={{0,2},{2,4},{4,6},{6,8},{8,10},{10,12},{12,14},{14,0},{1,3},{3,5},... | collective-permute-start | bytes 49160 | tf_op jit(solution)/shard_map/ppermute | solution.py:18
  206.8 8.4 %collective-permute-start.5 = (bf16[1,4,2,8,128]{4,3,1,2,0:T(8,128)(2,1)S(1)}, bf16[1,4,2,8,128]{4,3,1,2,0:T(8,128)(2,1)S(1)}, u32[]{:S(2)}, u32[]{:S(2)}) collective-permute-start(bf16[1,4,2,8,128]{4,3,1,2,0:T(8,128)(2,1)S(1)} %fusion.20), channel_id=1, source_target_pairs={{2,0},{4,2},{6,4},{8,6},{10,8},{12,10},{14,12},{0,14},{3,1},{5,3},... | collective-permute-start | bytes 49160 | tf_op jit(solution)/shard_map/ppermute | solution.py:19
  215.2 4.0 %copy-start.22 = (pred[4,9]{1,0:T(4,128)(4,1)S(1)}, pred[4,9]{1,0:T(4,128)(4,1)}, u32[]{:S(2)}) copy-start(pred[4,9]{1,0:T(4,128)(4,1)} %and_bitcast_fusion) | copy-start | bytes 112
  215.3 1.2 collective-permute-start.7
  215.9 1.3 collective-permute-start.6
  219.1 50.9 %copy-start.17 = (f32[8,1,1024]{2,0,1:T(8,128)S(1)}, f32[8,1,1024]{2,0,1:T(8,128)}, u32[]{:S(2)}) copy-start(f32[8,1,1024]{2,0,1:T(8,128)} %copy-done.16) | copy-start | bytes 98308
  291.7 3.8 %copy-start.11 = (bf16[512,128]{0,1:T(8,128)(2,1)S(1)}, bf16[512,128]{0,1:T(8,128)(2,1)}, u32[]{:S(2)}) copy-start(bf16[512,128]{0,1:T(8,128)(2,1)} %copy-done.9) | copy-start | bytes 393220
  298.4 1.4 copy-start.15
  (11 other events, 11.6 us)
Sparse Core Ops, SparseCore 0:
  58.1 54.7 reduce-scatter.2
  215.3 54.6 reduce-scatter.4
